TPU v7x, 256 devices: a whole 4x4x8 slice. The times are simulated.
256 devices in a mesh: dp: 2 (over core), row: 16 (over x, y), col: 8 (over z).
Axes of the slice: x: 4, y: 4, z: 8, core: 2. Of those that a mesh axis runs over, the one named last changes fastest.
Arguments:
- tokens: bfloat16 [768, 8192], P(('dp', 'col'), 'row'), may hold values from -160 to 160
- norm_gain: float32 [8192], P('row'), may hold values from 0.3 to 3
- gate_weight: bfloat16 [8192, 14336], P('row', ('dp', 'col')), may hold values from -0.0625 to 0.0625
- up_weight: bfloat16 [8192, 14336], P('row', ('dp', 'col')), may hold values from -0.0625 to 0.0625
- down_weight: bfloat16 [14336, 8192], P(('dp', 'col'), 'row'), may hold values from -0.046875 to 0.046875
- gate_keep: int32 [64, 112], P('row', ('dp', 'col')), may hold values from 0 to 1, as said below
- up_keep: int32 [64, 112], P('row', ('dp', 'col')), may hold values from 0 to 1, as said below
- down_keep: int32 [112, 64], P(('dp', 'col'), 'row'), may hold values from 0 to 1, as said below
- cotangent: bfloat16 [768, 8192], P(('dp', 'col'), 'row'), may hold values from -80 to 80
Outputs:
- branch: bfloat16 [768, 8192], P(('dp', 'col'), 'row')
- grad_tokens: float32 [768, 8192], P(('dp', 'col'), 'row')
- grad_gain: float32 [8192], P('row')
- grad_gate: float32 [8192, 14336], P('row', ('dp', 'col'))
- grad_up: float32 [8192, 14336], P('row', ('dp', 'col'))
- grad_down: float32 [14336, 8192], P(('dp', 'col'), 'row')
Inputs may be any that keep to these rules, and one draw needn't show every extreme that they name: `gate_keep`: 1 keeps a 128 x 128 block of the gate projection, 0 prunes it. `up_keep`: 1 keeps a 128 x 128 block of the up projection, 0 prunes it. `down_keep`: 1 keeps a 128 x 128 block of the down projection, 0 prunes it.
All inputs are finite; a program needn't handle non-finite values.
Results may differ from a plain program's by a relative error of at most 0.0065.
Values may be sent and summed in bfloat16 or wider, within the bound.
A program may use at most 128 MiB of HBM per device.

v0:
```python
import jax
import jax.numpy as jnp
from jax import lax
from jax.sharding import PartitionSpec as P

D = 8192
BLOCK = 128


def expand_keep(keep, target_type):
    return jnp.repeat(jnp.repeat(keep, BLOCK, axis=0), BLOCK, axis=1).astype(target_type)


def activate(gate, up_value):
    return (gate * jax.nn.sigmoid(gate) * up_value).astype(jnp.bfloat16)


def on_device(
    tokens, norm_gain, gate_weight, up_weight, down_weight, gate_keep, up_keep, down_keep, cotangent
):
    token_f = tokens.astype(jnp.float32)
    square = lax.psum(jnp.sum(token_f * token_f, axis=1), "row")
    inv_rms = lax.rsqrt(square[:, None] / D + 1e-05)
    normed = (token_f * inv_rms * norm_gain).astype(jnp.bfloat16)
    gate_masked = gate_weight * expand_keep(gate_keep, jnp.bfloat16)
    up_masked = up_weight * expand_keep(up_keep, jnp.bfloat16)
    down_masked = down_weight * expand_keep(down_keep, jnp.bfloat16)
    gate_full, up_full = (
        lax.all_gather(gate_masked, "dp", axis=1, tiled=True),
        lax.all_gather(up_masked, "dp", axis=1, tiled=True),
    )
    down_full = lax.all_gather(down_masked, "dp", axis=0, tiled=True)
    seen_rows = lax.all_gather(normed, "col", axis=0, tiled=True)
    seen_cot = lax.all_gather(cotangent, "col", axis=0, tiled=True)
    width_f = gate_full.shape[1]
    contract_last = (((1,), (1,)), ((), ()))
    contract_first = (((0,), (0,)), ((), ()))
    row_block = seen_rows
    summed = lax.psum_scatter(
        jnp.concatenate(
            [
                jnp.dot(row_block, gate_full, preferred_element_type=jnp.float32),
                jnp.dot(row_block, up_full, preferred_element_type=jnp.float32),
            ],
            axis=1,
        ),
        "row",
        scatter_dimension=0,
        tiled=True,
    )
    gate_part = summed[:, :width_f]
    up_part = summed[:, width_f:]
    hidden = lax.all_gather(activate(gate_part, up_part), "row", axis=0, tiled=True)
    row_block = hidden
    branch_sum = lax.psum_scatter(
        jnp.dot(row_block, down_full, preferred_element_type=jnp.float32),
        "col",
        scatter_dimension=0,
        tiled=True,
    )
    branch = branch_sum.astype(jnp.bfloat16)
    row_block = seen_cot
    hidden_grad = lax.psum_scatter(
        lax.dot_general(row_block, down_full, contract_last, preferred_element_type=jnp.float32),
        "row",
        scatter_dimension=0,
        tiled=True,
    )
    sigmoid_gate = jax.nn.sigmoid(gate_part)
    gate_grad = (
        hidden_grad * up_part * sigmoid_gate * (1.0 + gate_part * (1.0 - sigmoid_gate))
    ).astype(jnp.bfloat16)
    up_grad = (hidden_grad * gate_part * sigmoid_gate).astype(jnp.bfloat16)
    gate_grads, up_grads = (
        lax.all_gather(gate_grad, "row", axis=0, tiled=True),
        lax.all_gather(up_grad, "row", axis=0, tiled=True),
    )
    normed_grad = lax.psum_scatter(
        lax.dot_general(gate_grads, gate_full, contract_last, preferred_element_type=jnp.float32)
        + lax.dot_general(up_grads, up_full, contract_last, preferred_element_type=jnp.float32),
        "col",
        scatter_dimension=0,
        tiled=True,
    )
    down_local = lax.dot_general(
        hidden, seen_cot, contract_first, preferred_element_type=jnp.float32
    )
    gate_local = lax.dot_general(
        seen_rows, gate_grads, contract_first, preferred_element_type=jnp.float32
    )
    up_local = lax.dot_general(
        seen_rows, up_grads, contract_first, preferred_element_type=jnp.float32
    )
    gate_total, up_total = (
        lax.psum_scatter(gate_local, "dp", scatter_dimension=1, tiled=True),
        lax.psum_scatter(up_local, "dp", scatter_dimension=1, tiled=True),
    )
    down_total = lax.psum_scatter(down_local, "dp", scatter_dimension=0, tiled=True)
    grad_gate = gate_total * expand_keep(gate_keep, jnp.float32)
    grad_up = up_total * expand_keep(up_keep, jnp.float32)
    grad_down = down_total * expand_keep(down_keep, jnp.float32)
    grad_gain = lax.psum(jnp.sum(normed_grad * token_f * inv_rms, axis=0), ("dp", "col"))
    inner_dot = lax.psum(jnp.sum(norm_gain * normed_grad * token_f, axis=1), "row")
    grad_tokens = (
        inv_rms * norm_gain * normed_grad
        - token_f * inv_rms * inv_rms * inv_rms * inner_dot[:, None] / D
    )
    return (branch, grad_tokens, grad_gain, grad_gate, grad_up, grad_down)


def solution(mesh):
    in_specs = (
        P(("dp", "col"), "row"),
        P("row"),
        P("row", ("dp", "col")),
        P("row", ("dp", "col")),
        P(("dp", "col"), "row"),
        P("row", ("dp", "col")),
        P("row", ("dp", "col")),
        P(("dp", "col"), "row"),
        P(("dp", "col"), "row"),
    )
    out_specs = (
        P(("dp", "col"), "row"),
        P(("dp", "col"), "row"),
        P("row"),
        P("row", ("dp", "col")),
        P("row", ("dp", "col")),
        P(("dp", "col"), "row"),
    )
    return jax.shard_map(
        on_device, mesh=mesh, in_specs=in_specs, out_specs=out_specs, check_vma=False
    )
```

profile of v0, /device:TPU:1, one launch (start us, length us, event | category | flops | bytes accessed | tf_op | source)
XLA Modules:
  0.0 618.9 jit_solution(13454673228477233298)
XLA Ops:
  7.2 0.8 fusion.13
  8.0 0.1 copy.29
  8.1 0.1 broadcast_bitcast_fusion.3
  8.2 1.5 copy.30
  9.7 1.0 bitcast_multiply_fusion.3
  10.7 0.1 copy.31
  10.8 0.1 broadcast_bitcast_fusion.2
  10.9 0.2 copy-done.6
  11.2 0.5 copy.32
  11.7 1.0 bitcast_multiply_fusion.2
  12.8 0.1 copy.33
  12.9 1.1 broadcast_in_dim.46
  14.1 1.1 bitcast_multiply_fusion.1
  15.3 0.1 fusion.7
  15.4 34.2 %psum.21 = f32[48]{0:T(128)S(1)} all-reduce(f32[48]{0:T(128)S(1)} %fusion.7), channel_id=1, replica_groups=mesh['dp'=2,'row'=16,'col'=8] {'row'}, use_global_device_ids=true, to_apply=%region_1.0 | all-reduce | flops 48 | bytes 384 | tf_op jit(solution)/shard_map/psum | solution.py:22
  49.6 0.6 copy-done.12
  50.2 0.1 fusion.2
  50.3 22.6 %all_gather.24 = bf16[384,512]{1,0:T(8,128)(2,1)S(1)} all-gather(bf16[48,512]{1,0:T(8,128)(2,1)S(1)} %fusion.2), channel_id=1, replica_groups=mesh['dp'=2,'row'=16,'col'=8] {'col'}, dimensions={0}, use_global_device_ids=true | all-gather | bytes 442368 | tf_op jit(solution)/shard_map/all_gather | solution.py:33
  72.9 2.4 fusion.14
  75.3 2.4 fusion.15
  77.7 3.2 pad_maximum_fusion
  81.0 0.7 copy-done.10
  81.7 19.5 %all_gather.29 = bf16[384,512]{1,0:T(8,128)(2,1)S(1)} all-gather(bf16[48,512]{1,0:T(8,128)(2,1)S(1)} %copy-done.10), channel_id=1, replica_groups=mesh['dp'=2,'row'=16,'col'=8] {'col'}, dimensions={0}, use_global_device_ids=true | all-gather | bytes 442368 | tf_op jit(solution)/shard_map/all_gather | solution.py:34
  101.3 2.6 convolution_bitcast_fusion
  103.9 2.3 copy.34
  106.3 0.6 copy-done.16
  106.9 0.6 dynamic-slice
  108.1 105.8 %all-reduce.4.cloned.1.call-done = f32[384,3584]{1,0:T(8,128)} async-done(((f32[384,3584]{1,0:T(8,128)}), f32[384,3584]{1,0:T(8,128)}) %all-reduce.4.cloned.1.call-update) | async-done | bytes 5505040
  213.9 83.0 %reduce-scatter.19.cloned.1.call-done = f32[24,1792]{1,0:T(8,128)} async-done(((f32[384,1792]{1,0:T(8,128)}), f32[24,1792]{1,0:T(8,128)}) %reduce-scatter.19.cloned.1.call-update) | async-done | bytes 172048
  297.0 1.9 multiply_convert_fusion
  298.9 0.7 all-gather.15.cloned.1.call-update
  299.7 0.7 all-gather.17.cloned.1.call-update
  300.4 46.9 %all-gather.11.cloned.1.call-done = bf16[384,1792]{1,0:T(8,128)(2,1)} async-done(((bf16[24,1792]{1,0:T(8,128)(2,1)}), bf16[384,1792]{1,0:T(8,128)(2,1)}) %all-gather.11.cloned.1.call-update) | async-done | bytes 1376272 | tf_op jit(solution)/shard_map/all_gather | solution.py:53
  347.3 3.1 fusion.16
  350.5 47.7 %all-gather.15.cloned.1.call-done = bf16[384,1792]{1,0:T(8,128)(2,1)} async-done(((bf16[24,1792]{1,0:T(8,128)(2,1)}), bf16[384,1792]{1,0:T(8,128)(2,1)}) %all-gather.15.cloned.1.call-update) | async-done | bytes 1376272 | tf_op jit(solution)/shard_map/all_gather | solution.py:75
  398.2 2.8 fusion.17
  401.0 48.1 %all-gather.17.cloned.1.call-done = bf16[384,1792]{1,0:T(8,128)(2,1)} async-done(((bf16[24,1792]{1,0:T(8,128)(2,1)}), bf16[384,1792]{1,0:T(8,128)(2,1)}) %all-gather.17.cloned.1.call-update) | async-done | bytes 1376272 | tf_op jit(solution)/shard_map/all_gather | solution.py:76
  449.1 3.1 convolution_add_fusion
  452.3 4.3 fusion.18
  456.6 1.3 copy-done.5
  457.9 3.0 fusion.19
  460.9 1.3 copy-done.2
  462.2 3.1 fusion.20
  465.3 0.1 copy.35
  465.4 0.1 broadcast_bitcast_fusion.1
  465.5 0.2 broadcast_in_dim.48
  465.7 1.7 copy.36
  467.4 0.1 copy.37
  467.5 0.1 broadcast_bitcast_fusion
  467.6 0.2 broadcast_in_dim.50
  467.8 1.7 copy.38
  469.5 0.1 copy.39
  469.6 17.5 %reduce-scatter.9.cloned.1.call-done = f32[48,512]{1,0:T(8,128)} async-done(((f32[384,512]{1,0:T(8,128)}), f32[48,512]{1,0:T(8,128)}) %reduce-scatter.9.cloned.1.call-update) | async-done | bytes 98320 | tf_op jit(solution)/shard_map/reduce_scatter | solution.py:55
  487.1 1.5 convert_element_type.96
  488.6 37.9 %reduce-scatter.11.cloned.1.call-done = f32[48,512]{1,0:T(8,128)} async-done(((f32[384,512]{1,0:T(8,128)}), f32[48,512]{1,0:T(8,128)}) %reduce-scatter.11.cloned.1.call-update) | async-done | bytes 98320 | tf_op jit(solution)/shard_map/reduce_scatter | solution.py:78
  526.5 1.1 fusion.10
  527.5 33.1 %psum.22 = f32[48]{0:T(128)S(1)} all-reduce(f32[48]{0:T(128)S(1)} %get-tuple-element.7), channel_id=1, replica_groups=mesh['dp'=2,'row'=16,'col'=8] {'row'}, use_global_device_ids=true, to_apply=%region_7.0 | all-reduce | flops 48 | bytes 384 | tf_op jit(solution)/shard_map/psum | solution.py:103
  560.6 40.5 %psum.23 = f32[512]{0:T(512)} all-reduce(f32[512]{0:T(512)S(1)} %get-tuple-element.6), channel_id=1, replica_groups=mesh['dp'=2,'row'=16,'col'=8] {'dp','col'}, use_global_device_ids=true, to_apply=%region_9.0 | all-reduce | flops 512 | bytes 4096 | tf_op jit(solution)/shard_map/psum | solution.py:102
  601.1 1.6 fusion.6
  602.7 3.6 mul.141
  606.3 2.9 mul.142
  609.3 1.1 broadcast_in_dim.52
  610.4 0.4 copy-done.4
  610.8 1.6 bitcast_multiply_fusion
  (66 shorter events, 0.9 us)
Async XLA Ops:
  7.2 65.7 %all-gather.7.cloned.1.call-start = ((), (), s32[]{:S(2)}) async-start(), calls=%async_computation.6 | async-start | bytes 2752512 | tf_op jit(solution)/shard_map/all_gather | solution.py:29
  9.6 1.1 copy-start.14
  9.6 1.5 copy-start.6
  10.7 64.7 %all-gather.9.cloned.1.call-start = ((), (), s32[]{:S(2)}) async-start(), calls=%async_computation.7 | async-start | bytes 2752512 | tf_op jit(solution)/shard_map/all_gather | solution.py:30
  11.7 1.1 copy-start.15
  11.7 2.4 copy-start.7
  12.7 88.6 %all-gather.13.cloned.1.call-start = ((), (), s32[]{:S(2)}) async-start(), calls=%async_computation.9 | async-start | bytes 2752512 | tf_op jit(solution)/shard_map/all_gather | solution.py:32
  14.1 1.2 copy-start.8
  14.1 36.1 %copy-start.11 = (f32[512]{0:T(512)S(1)}, f32[512]{0:T(512)}, u32[]{:S(2)}) copy-start(f32[512]{0:T(512)} %param.10) | copy-start | bytes 6148
  15.2 198.7 %all-reduce.4.cloned.1.call-start = ((), (), s32[]{:S(2)}) async-start(), calls=%async_computation.17 | async-start | bytes 11010048
  49.6 0.6 copy-start.12
  80.9 0.8 copy-start.10
  81.0 216.0 %reduce-scatter.19.cloned.1.call-start = ((), (), s32[]{:S(2)}) async-start(), calls=%async_computation.18 | async-start | bytes 2924544
  106.2 0.7 copy-start.16
  106.2 241.1 %copy-start.1 = (bf16[1792,512]{1,0:T(8,128)(2,1)S(1)}, bf16[1792,512]{1,0:T(8,128)(2,1)}, u32[]{:S(2)}) copy-start(bf16[1792,512]{1,0:T(8,128)(2,1)} %all-gather.13.cloned.1.call-done) | copy-start | bytes 5505028
  106.2 241.1 %all-gather.11.cloned.1.call-start = ((), (), s32[]{:S(2)}) async-start(), calls=%async_computation.8 | async-start | bytes 1462272 | tf_op jit(solution)/shard_map/all_gather | solution.py:53
  298.9 99.3 %all-gather.15.cloned.1.call-start = ((), (), s32[]{:S(2)}) async-start(), calls=%async_computation.11 | async-start | bytes 1462272 | tf_op jit(solution)/shard_map/all_gather | solution.py:75
  299.6 149.4 %all-gather.17.cloned.1.call-start = ((), (), s32[]{:S(2)}) async-start(), calls=%async_computation.12 | async-start | bytes 1462272 | tf_op jit(solution)/shard_map/all_gather | solution.py:76
  300.4 186.7 %reduce-scatter.9.cloned.1.call-start = ((), (), s32[]{:S(2)}) async-start(), calls=%async_computation.10 | async-start | bytes 884736 | tf_op jit(solution)/shard_map/reduce_scatter | solution.py:55
  350.5 98.6 %copy-start.3 = (bf16[512,1792]{0,1:T(8,128)(2,1)S(1)}, bf16[512,1792]{0,1:T(8,128)(2,1)}, u32[]{:S(2)}) copy-start(bf16[512,1792]{0,1:T(8,128)(2,1)} %all-gather.9.cloned.1.call-done) | copy-start | bytes 5505028
  350.5 176.0 %reduce-scatter.11.cloned.1.call-start = ((), (), s32[]{:S(2)}) async-start(), calls=%async_computation.13 | async-start | bytes 884736 | tf_op jit(solution)/shard_map/reduce_scatter | solution.py:78
  452.2 150.5 %reduce-scatter.13.cloned.1.call-start = ((), (), s32[]{:S(2)}) async-start(), calls=%async_computation.14 | async-start | bytes 5505024 | tf_op jit(solution)/shard_map/reduce_scatter | solution.py:95
  456.5 1.3 copy-start.5
  456.6 149.8 %reduce-scatter.15.cloned.1.call-start = ((), (), s32[]{:S(2)}) async-start(), calls=%async_computation.15 | async-start | bytes 5505024 | tf_op jit(solution)/shard_map/reduce_scatter | solution.py:96
  460.9 1.3 copy-start.2
  460.9 148.4 %reduce-scatter.17.cloned.1.call-start = ((), (), s32[]{:S(2)}) async-start(), calls=%async_computation.16 | async-start | bytes 5505024 | tf_op jit(solution)/shard_map/reduce_scatter | solution.py:98
  467.8 58.7 %copy-start.9 = (bf16[48,512]{1,0:T(8,128)(2,1)S(1)}, bf16[48,512]{1,0:T(8,128)(2,1)}, u32[]{:S(2)}) copy-start(bf16[48,512]{1,0:T(8,128)(2,1)} %param.9) | copy-start | bytes 147460
  467.8 58.7 %copy-start.13 = (f32[48]{0:T(128)S(1)}, f32[48]{0:T(128)}, u32[]{:S(2)}) copy-start(f32[48]{0:T(128)} %copy-done.12) | copy-start | bytes 580
  602.7 3.6 copy-start
  609.3 1.5 copy-start.4
Sparse Core Ops, SparseCore 0:
  10.8 20.0 all-gather.6
  33.2 16.8 all-gather.8
  52.5 16.8 all-gather.12
  81.1 132.8 all-reduce.3
  217.4 79.5 reduce-scatter.18
  299.9 47.4 all-gather.10
  350.4 47.7 all-gather.14
  401.3 47.7 all-gather.16
  452.2 34.8 reduce-scatter.8
  489.5 36.9 reduce-scatter.10
  529.0 20.7 reduce-scatter.12
  552.1 18.3 reduce-scatter.14
  573.0 18.6 reduce-scatter.16
where the time goes:
time: 620 us; the launch traced here: 619 us
  waiting for transfers between devices  388 us (63%)
  blocking collectives  150 us (24%)
  matrix products  26.8 us (4%)
  other arithmetic  21.5 us (3%)
  local copies, waits for them, and re-layouts  17 us (3%)
  between operations  14.8 us (2%)
    unnamed x15, waiting for transfers between devices  190 us
    all_gather x1, waiting for transfers between devices, on_device(): lax.all_gather(up_grad, 'row', axis=0, tiled=True)  48.1 us
    all_gather x1, waiting for transfers between devices, on_device(): lax.all_gather(gate_grad, 'row', axis=0, tiled=True)  47.7 us
    all_gather x1, waiting for transfers between devices, on_device(): lax.all_gather(activate(gate_part, up_part), 'row', axis=0, tiled=True)  46.9 us
    psum x1, blocking collectives, on_device(): lax.psum(jnp.sum(normed_grad * token_f * inv_rms, axis=0), ('dp', 'col'))  40.5 us
    reduce_scatter x1, waiting for transfers between devices, on_device(): lax.psum_scatter(lax.dot_general(gate_grads, gate_full, contract_last, pr...  37.9 us
    psum x1, blocking collectives, on_device(): square = lax.psum(jnp.sum(token_f * token_f, axis=1), 'row')  34.2 us
    psum x1, blocking collectives, on_device(): lax.psum(jnp.sum(norm_gain * normed_grad * token_f, axis=1), 'row')  33.1 us
  transfers between devices with their start and end apart: 13, of which 7 were waited for; matrix products, arithmetic and copies ran while one was open for 8% of the time, Pallas kernels for 0%

commit v1 on v0

--- a/solution.py
+++ b/solution.py
@@ -5,6 +5,12 @@
 
 D = 8192
 BLOCK = 128
+
+
+def expand_the_boxes(tile_in):
+    return jnp.concatenate(
+        lax.all_to_all(jnp.stack(lax.axis_size("row") * [tile_in]), "row", 0, 0), axis=0
+    )
 
 
 def expand_keep(keep, target_type):
@@ -73,7 +79,7 @@
     up_grad = (hidden_grad * gate_part * sigmoid_gate).astype(jnp.bfloat16)
     gate_grads, up_grads = (
         lax.all_gather(gate_grad, "row", axis=0, tiled=True),
-        lax.all_gather(up_grad, "row", axis=0, tiled=True),
+        expand_the_boxes(up_grad),
     )
     normed_grad = lax.psum_scatter(
         lax.dot_general(gate_grads, gate_full, contract_last, preferred_element_type=jnp.float32)

time: 620 us -> 575 us (0.927)
  waiting for transfers between devices: 388 us -> 338 us
    all_gather x1 -> x0, waiting for transfers between devices: 48.1 us -> none  [on_device(): lax.all_gather(up_grad, 'row', axis=0, tiled=True)]
    unnamed x15 -> x14, waiting for transfers between devices: 190 us -> 190 us
  transfers between devices with their start and end apart: 13 -> 13, of which waited for: 7 -> 6; matrix products, arithmetic and copies ran while one was open for 8% -> 9% of each run, Pallas kernels for 0% -> 0%
where the time goes in v1:
time: 575 us; the launch traced here: 574 us
  waiting for transfers between devices  338 us (59%)
  blocking collectives  150 us (26%)
  matrix products  26.1 us (5%)
  other arithmetic  21.5 us (4%)
  local copies, waits for them, and re-layouts  18.2 us (3%)
  between operations  15.1 us (3%)
    unnamed x14, waiting for transfers between devices  190 us
    all_gather x1, waiting for transfers between devices, on_device(): lax.all_gather(activate(gate_part, up_part), 'row', axis=0, tiled=True)  47.3 us
    all_gather x1, waiting for transfers between devices, on_device(): lax.all_gather(gate_grad, 'row', axis=0, tiled=True)  47.1 us
    psum x1, blocking collectives, on_device(): lax.psum(jnp.sum(normed_grad * token_f * inv_rms, axis=0), ('dp', 'col'))  40.6 us
    reduce_scatter x1, waiting for transfers between devices, on_device(): lax.psum_scatter(lax.dot_general(gate_grads, gate_full, contract_last, pr...  38 us
    psum x1, blocking collectives, on_device(): square = lax.psum(jnp.sum(token_f * token_f, axis=1), 'row')  34.2 us
    psum x1, blocking collectives, on_device(): lax.psum(jnp.sum(norm_gain * normed_grad * token_f, axis=1), 'row')  33.1 us
    all_gather x1, blocking collectives, on_device(): seen_rows = lax.all_gather(normed, 'col', axis=0, tiled=True)  22.6 us
  transfers between devices with their start and end apart: 13, of which 6 were waited for; matrix products, arithmetic and copies ran while one was open for 9% of the time, Pallas kernels for 0%

profile of v1, /device:TPU:1, one launch (start us, length us, event | category | flops | bytes accessed | tf_op | source)
XLA Modules:
  0.0 573.8 jit_solution(18029155657272158399)
XLA Ops:
  7.2 0.8 fusion.13
  8.0 0.1 copy.29
  8.1 0.1 broadcast_bitcast_fusion.3
  8.2 1.5 copy.30
  9.7 1.0 bitcast_multiply_fusion.3
  10.7 0.1 copy.31
  10.8 0.1 broadcast_bitcast_fusion.2
  10.9 0.2 copy-done.4
  11.2 0.5 copy.32
  11.7 1.0 bitcast_multiply_fusion.2
  12.8 0.1 copy.33
  12.9 1.1 broadcast_in_dim.46
  14.1 1.1 bitcast_multiply_fusion.1
  15.3 0.1 fusion.7
  15.4 34.2 %psum.21 = f32[48]{0:T(128)S(1)} all-reduce(f32[48]{0:T(128)S(1)} %fusion.7), channel_id=1, replica_groups=mesh['dp'=2,'row'=16,'col'=8] {'row'}, use_global_device_ids=true, to_apply=%region_1.0 | all-reduce | flops 48 | bytes 384 | tf_op jit(solution)/shard_map/psum | solution.py:28
  49.6 0.6 copy-done.10
  50.2 0.1 fusion.2
  50.3 22.6 %all_gather.21 = bf16[384,512]{1,0:T(8,128)(2,1)S(1)} all-gather(bf16[48,512]{1,0:T(8,128)(2,1)S(1)} %fusion.2), channel_id=1, replica_groups=mesh['dp'=2,'row'=16,'col'=8] {'col'}, dimensions={0}, use_global_device_ids=true | all-gather | bytes 442368 | tf_op jit(solution)/shard_map/all_gather | solution.py:39
  72.9 2.4 fusion.14
  75.3 2.4 fusion.15
  77.8 3.2 pad_maximum_fusion
  81.0 0.7 copy-done.8
  81.7 19.6 %all_gather.26 = bf16[384,512]{1,0:T(8,128)(2,1)S(1)} all-gather(bf16[48,512]{1,0:T(8,128)(2,1)S(1)} %copy-done.8), channel_id=1, replica_groups=mesh['dp'=2,'row'=16,'col'=8] {'col'}, dimensions={0}, use_global_device_ids=true | all-gather | bytes 442368 | tf_op jit(solution)/shard_map/all_gather | solution.py:40
  101.3 2.6 convolution_bitcast_fusion
  103.9 2.3 copy.34
  106.4 0.6 copy-done.14
  107.0 0.6 dynamic-slice
  108.2 105.7 %all-reduce.4.cloned.1.call-done = f32[384,3584]{1,0:T(8,128)} async-done(((f32[384,3584]{1,0:T(8,128)}), f32[384,3584]{1,0:T(8,128)}) %all-reduce.4.cloned.1.call-update) | async-done | bytes 5505040
  213.9 83.0 %reduce-scatter.19.cloned.1.call-done = f32[24,1792]{1,0:T(8,128)} async-done(((f32[384,1792]{1,0:T(8,128)}), f32[24,1792]{1,0:T(8,128)}) %reduce-scatter.19.cloned.1.call-update) | async-done | bytes 172048
  297.0 1.9 multiply_convert_fusion
  298.9 0.7 all-gather.14.cloned.1.call-update
  299.6 1.2 stack.2
  300.8 4.4 all-to-all-start
  305.2 47.3 %all-gather.10.cloned.1.call-done = bf16[384,1792]{1,0:T(8,128)(2,1)} async-done(((bf16[24,1792]{1,0:T(8,128)(2,1)}), bf16[384,1792]{1,0:T(8,128)(2,1)}) %all-gather.10.cloned.1.call-update) | async-done | bytes 1376272 | tf_op jit(solution)/shard_map/all_gather | solution.py:59
  352.5 3.7 fusion.16
  356.3 47.1 %all-gather.14.cloned.1.call-done = bf16[384,1792]{1,0:T(8,128)(2,1)} async-done(((bf16[24,1792]{1,0:T(8,128)(2,1)}), bf16[384,1792]{1,0:T(8,128)(2,1)}) %all-gather.14.cloned.1.call-update) | async-done | bytes 1376272 | tf_op jit(solution)/shard_map/all_gather | solution.py:81
  403.4 2.8 fusion.17
  406.2 3.3 convolution_add_fusion
  409.6 2.9 fusion.19
  412.6 1.3 copy-done.3
  413.8 3.0 fusion.18
  416.9 1.3 copy-done.1
  418.1 3.1 fusion.20
  421.2 0.1 copy.37
  421.3 0.1 broadcast_bitcast_fusion
  421.4 0.2 broadcast_in_dim.50
  421.6 1.7 copy.38
  423.3 0.1 copy.35
  423.4 0.1 broadcast_bitcast_fusion.1
  423.5 0.2 broadcast_in_dim.48
  423.8 1.7 copy.36
  425.4 0.1 copy.39
  425.5 15.9 %reduce-scatter.9.cloned.1.call-done = f32[48,512]{1,0:T(8,128)} async-done(((f32[384,512]{1,0:T(8,128)}), f32[48,512]{1,0:T(8,128)}) %reduce-scatter.9.cloned.1.call-update) | async-done | bytes 98320 | tf_op jit(solution)/shard_map/reduce_scatter | solution.py:61
  441.4 1.5 convert_element_type.96
  442.9 38.0 %reduce-scatter.11.cloned.1.call-done = f32[48,512]{1,0:T(8,128)} async-done(((f32[384,512]{1,0:T(8,128)}), f32[48,512]{1,0:T(8,128)}) %reduce-scatter.11.cloned.1.call-update) | async-done | bytes 98320 | tf_op jit(solution)/shard_map/reduce_scatter | solution.py:84
  480.9 1.1 fusion.10
  482.0 33.1 %psum.22 = f32[48]{0:T(128)S(1)} all-reduce(f32[48]{0:T(128)S(1)} %get-tuple-element.7), channel_id=1, replica_groups=mesh['dp'=2,'row'=16,'col'=8] {'row'}, use_global_device_ids=true, to_apply=%region_7.0 | all-reduce | flops 48 | bytes 384 | tf_op jit(solution)/shard_map/psum | solution.py:109
  515.1 40.6 %psum.23 = f32[512]{0:T(512)} all-reduce(f32[512]{0:T(512)S(1)} %get-tuple-element.6), channel_id=1, replica_groups=mesh['dp'=2,'row'=16,'col'=8] {'dp','col'}, use_global_device_ids=true, to_apply=%region_9.0 | all-reduce | flops 512 | bytes 4096 | tf_op jit(solution)/shard_map/psum | solution.py:108
  555.7 1.6 fusion.6
  557.3 3.6 mul.142
  560.9 2.9 mul.141
  563.9 1.1 broadcast_in_dim.52
  565.0 0.4 copy-done.2
  565.3 1.6 bitcast_multiply_fusion
  (62 shorter events, 0.9 us)
Async XLA Ops:
  7.2 65.7 %all-gather.6.cloned.1.call-start = ((), (), s32[]{:S(2)}) async-start(), calls=%async_computation.7 | async-start | bytes 2752512 | tf_op jit(solution)/shard_map/all_gather | solution.py:35
  9.6 1.1 copy-start.12
  9.6 1.5 copy-start.4
  10.7 64.7 %all-gather.8.cloned.1.call-start = ((), (), s32[]{:S(2)}) async-start(), calls=%async_computation.8 | async-start | bytes 2752512 | tf_op jit(solution)/shard_map/all_gather | solution.py:36
  11.7 1.1 copy-start.13
  11.7 2.4 copy-start.5
  12.7 88.6 %all-gather.12.cloned.1.call-start = ((), (), s32[]{:S(2)}) async-start(), calls=%async_computation.10 | async-start | bytes 2752512 | tf_op jit(solution)/shard_map/all_gather | solution.py:38
  14.1 1.2 copy-start.6
  14.1 36.1 %copy-start.9 = (f32[512]{0:T(512)S(1)}, f32[512]{0:T(512)}, u32[]{:S(2)}) copy-start(f32[512]{0:T(512)} %param.10) | copy-start | bytes 6148
  15.2 198.7 %all-reduce.4.cloned.1.call-start = ((), (), s32[]{:S(2)}) async-start(), calls=%async_computation.17 | async-start | bytes 11010048
  49.6 0.6 copy-start.10
  80.9 0.8 copy-start.8
  81.0 216.0 %reduce-scatter.19.cloned.1.call-start = ((), (), s32[]{:S(2)}) async-start(), calls=%async_computation.18 | async-start | bytes 2924544
  106.3 0.7 copy-start.14
  106.3 246.2 %all-gather.10.cloned.1.call-start = ((), (), s32[]{:S(2)}) async-start(), calls=%async_computation.9 | async-start | bytes 1462272 | tf_op jit(solution)/shard_map/all_gather | solution.py:59
  298.9 104.6 %all-gather.14.cloned.1.call-start = ((), (), s32[]{:S(2)}) async-start(), calls=%async_computation.12 | async-start | bytes 1462272 | tf_op jit(solution)/shard_map/all_gather | solution.py:81
  300.8 105.4 %all-to-all-start = ((bf16[16,24,1792]{2,1,0:T(8,128)(2,1)}), bf16[16,24,1792]{2,1,0:T(8,128)(2,1)S(1)}, u32[]{:S(2)}, u32[]{:S(2)}) async-start(bf16[16,24,1792]{2,1,0:T(8,128)(2,1)} %stack.2), calls=%async_computation.1 | async-start | bytes 2752512 | tf_op jit(solution)/shard_map/all_to_all | solution.py:12
  305.2 136.2 %reduce-scatter.9.cloned.1.call-start = ((), (), s32[]{:S(2)}) async-start(), calls=%async_computation.11 | async-start | bytes 884736 | tf_op jit(solution)/shard_map/reduce_scatter | solution.py:61
  356.2 124.7 %reduce-scatter.11.cloned.1.call-start = ((), (), s32[]{:S(2)}) async-start(), calls=%async_computation.13 | async-start | bytes 884736 | tf_op jit(solution)/shard_map/reduce_scatter | solution.py:84
  409.5 147.8 %reduce-scatter.15.cloned.1.call-start = ((), (), s32[]{:S(2)}) async-start(), calls=%async_computation.15 | async-start | bytes 5505024 | tf_op jit(solution)/shard_map/reduce_scatter | solution.py:102
  412.5 1.3 copy-start.3
  412.5 148.4 %reduce-scatter.13.cloned.1.call-start = ((), (), s32[]{:S(2)}) async-start(), calls=%async_computation.14 | async-start | bytes 5505024 | tf_op jit(solution)/shard_map/reduce_scatter | solution.py:101
  416.8 1.3 copy-start.1
  416.8 147.0 %reduce-scatter.17.cloned.1.call-start = ((), (), s32[]{:S(2)}) async-start(), calls=%async_computation.16 | async-start | bytes 5505024 | tf_op jit(solution)/shard_map/reduce_scatter | solution.py:104
  423.7 57.2 %copy-start.7 = (bf16[48,512]{1,0:T(8,128)(2,1)S(1)}, bf16[48,512]{1,0:T(8,128)(2,1)}, u32[]{:S(2)}) copy-start(bf16[48,512]{1,0:T(8,128)(2,1)} %param.9) | copy-start | bytes 147460
  423.7 57.2 %copy-start.11 = (f32[48]{0:T(128)S(1)}, f32[48]{0:T(128)}, u32[]{:S(2)}) copy-start(f32[48]{0:T(128)} %copy-done.10) | copy-start | bytes 580
  557.3 3.6 copy-start
  563.8 1.5 copy-start.2
Sparse Core Ops, SparseCore 0:
  10.8 20.0 all-gather.5
  33.2 16.8 all-gather.7
  52.5 16.8 all-gather.11
  81.1 132.7 all-reduce.3
  217.4 79.5 reduce-scatter.18
  299.9 52.6 all-gather.9
  355.6 47.7 all-gather.13
  406.5 34.8 reduce-scatter.8
  443.9 36.9 reduce-scatter.10
  483.3 20.7 reduce-scatter.14
  506.5 18.3 reduce-scatter.12
  527.3 18.6 reduce-scatter.16
